TPU v7x, 32 devices: a whole 2x2x4 slice. The times are simulated.
32 devices in a mesh: chan: 16 (over z, y, core), slot: 2 (over x).
Axes of the slice: x: 2, y: 2, z: 4, core: 2. Of those that a mesh axis runs over, the one named last changes fastest.
Arguments:
- measured_real: float32 [2, 16, 1770], P('slot', 'chan'), may hold values from -60 to 60
- measured_imaginary: float32 [2, 16, 1770], P('slot', 'chan'), may hold values from -60 to 60
- measured_weight: float32 [2, 16, 1770], P('slot', 'chan'), may hold values from 0.3 to 3
- baseline_vectors: float32 [2, 3, 1770], P('slot'), may hold values from -120 to 120
- antenna_pairs: int32 [2, 1770], replicated, may hold values from 0 to 59, as said below
- directions: float32 [3, 200], replicated, may hold values from -0.12 to 0.12
- direction_flux: float32 [16, 200], P('chan'), may hold values from 0.2 to 2
- channel_frequency: float32 [16], P('chan'), may hold values from 1.1 to 1.9
- electron_content_start: float32 [2, 60, 200], P('slot'), may hold values from -6 to 6
- pierce_station_direction: int32 [2, 12000], P('slot'), may hold values from 0 to 11999, each once within a row
- eigen_basis: float32 [12000, 2048], P('chan'), may hold values from -0.0546875 to 0.0546875
- eigen_weight: float32 [2048], replicated, may hold values from 0.1 to 1
Outputs:
- tec_final: float32 [2, 60, 200], P('slot')
- coefficients: float32 [2, 2048], P('slot')
- final_residual_real: float32 [2, 16, 1770], P('slot', 'chan')
- final_residual_imaginary: float32 [2, 16, 1770], P('slot', 'chan')
Inputs may be any that keep to these rules, and one draw needn't show every extreme that they name: `antenna_pairs`: each column is a pair of two different stations, and the 1770 columns hold every unordered pair of stations exactly once. `pierce_station_direction`: each row names every station-direction pair exactly once.
All inputs are finite; a program needn't handle non-finite values.
Results may differ from a plain program's by a relative error of at most 0.00018.
Values sent between devices are 32-bit elements; how exact they have to be, the bound alone decides.
A program may use at most 64 MiB of HBM per device.

v0:
```python
import jax
import jax.numpy as jnp
from jax import lax
from jax.sharding import PartitionSpec as P

ITERS = 4
HIGHEST = lax.Precision.HIGHEST
TEC_PHASE = -0.8448
SMOOTHING = 0.5
TWO_PI = 6.283185307179586


def padded_2(cells, sides, width):
    for axis, dim in sides:
        count = lax.axis_size(axis)
        ends = count - 1
        head = lax.slice_in_dim(cells, 0, width, axis=dim)
        tail = lax.slice_in_dim(cells, cells.shape[dim] - width, cells.shape[dim], axis=dim)
        cells = jnp.concatenate(
            [
                lax.ppermute(tail, axis, [(i, (i + 1) % count) for i in range(ends)]),
                cells,
                lax.ppermute(head, axis, [((i + 1) % count, i) for i in range(ends)]),
            ],
            axis=dim,
        )
    return cells


def station_polarity(antenna_pairs, station_list):
    station_numbers = jnp.arange(station_list, dtype=jnp.int32)[:, None]
    first_match = (antenna_pairs[0][None, :] == station_numbers).astype(jnp.float32)
    second_match = (antenna_pairs[1][None, :] == station_numbers).astype(jnp.float32)
    return (first_match - second_match, first_match + second_match)


def pair_terms(
    vis_real, vis_imag, weights, coords, frequency, fluxes, tec_slot, signed_terms, directions
):
    geometry = TWO_PI * frequency * jnp.dot(coords.T, directions, precision=HIGHEST)
    station_phase = TEC_PHASE / frequency * tec_slot
    phases = geometry + jnp.dot(signed_terms.T, station_phase, precision=HIGHEST)
    model_real = fluxes[None, :] * jnp.cos(phases)
    model_imag = fluxes[None, :] * jnp.sin(phases)
    leftover_real = vis_real - jnp.sum(model_real, axis=1)
    leftover_imaginary = vis_imag - jnp.sum(model_imag, axis=1)
    projected = weights[:, None] * (
        model_real * leftover_imaginary[:, None] - model_imag * leftover_real[:, None]
    )
    numerator = TEC_PHASE / frequency * jnp.dot(signed_terms, projected, precision=HIGHEST)
    return (numerator, leftover_real, leftover_imaginary)


def slot_smooth(values, padded):
    shard_slots = values.shape[0]
    first_slot = lax.axis_index("slot") * shard_slots
    position = first_slot + jnp.arange(shard_slots, dtype=jnp.int32)
    slot_total = shard_slots * lax.axis_size("slot")
    neighbours = (position > 0).astype(jnp.float32) + (position < slot_total - 1).astype(
        jnp.float32
    )
    return (values + SMOOTHING * (padded[:-2] + padded[2:])) / (1.0 + SMOOTHING * neighbours)[
        :, None
    ]


def smooth_coefficients(values):
    padded = padded_2(values, (("slot", 0),), 1)
    return slot_smooth(values, padded)


def reduce_normals(values):
    return lax.psum(values, "chan")


def updated_field(tec_flat, numer_sum, denom_sum):
    return tec_flat + numer_sum / denom_sum


def select_points(field, one_station, one_direction):
    rows = jnp.einsum("trs,tsd->trd", one_station, field, precision=HIGHEST)
    return jnp.sum(rows * one_direction, axis=2)


def place_points(values, one_station, one_direction):
    return jnp.einsum(
        "trs,trd->tsd", one_station, values[:, :, None] * one_direction, precision=HIGHEST
    )


def per_device(
    measured_real,
    measured_imaginary,
    measured_weight,
    baseline_vectors,
    antenna_pairs,
    directions,
    direction_flux,
    channel_frequency,
    electron_content_start,
    pierce_station_direction,
    eigen_basis,
    eigen_weight,
):
    shard_slots, shard_channels, baseline_list = measured_real.shape
    station_list = electron_content_start.shape[1]
    sources = electron_content_start.shape[2]
    block_rows = eigen_basis.shape[0]
    signed_terms, station_touches = station_polarity(antenna_pairs, station_list)
    tec_scale = TEC_PHASE / channel_frequency
    station_weight = jnp.einsum("sb,tfb->tfs", station_touches, measured_weight, precision=HIGHEST)
    denominator = jnp.einsum(
        "tfs,fd->tsd",
        station_weight * (tec_scale * tec_scale)[None, :, None],
        direction_flux * direction_flux,
        precision=HIGHEST,
    )
    own_map = lax.dynamic_slice_in_dim(
        pierce_station_direction, lax.axis_index("chan") * block_rows, block_rows, 1
    )
    station_of = own_map // sources
    direction_of = own_map % sources
    one_station = (
        station_of[:, :, None] == jnp.arange(station_list, dtype=jnp.int32)[None, None, :]
    ).astype(jnp.float32)
    one_direction = (
        direction_of[:, :, None] == jnp.arange(sources, dtype=jnp.int32)[None, None, :]
    ).astype(jnp.float32)
    denom_sum = reduce_normals(denominator.reshape(shard_slots, -1))
    tec_flat = electron_content_start.reshape(shard_slots, -1)
    pair_total = shard_slots * shard_channels
    smooth = None
    leftover_real = None
    leftover_imaginary = None
    for iteration in range(ITERS):
        current = tec_flat

        def pair_step(flat_index):
            slot_index = flat_index // shard_channels
            channel = flat_index % shard_channels
            tec_slot = current[slot_index].reshape(station_list, sources)
            return pair_terms(
                measured_real[slot_index, channel],
                measured_imaginary[slot_index, channel],
                measured_weight[slot_index, channel],
                baseline_vectors[slot_index],
                channel_frequency[channel],
                direction_flux[channel],
                tec_slot,
                signed_terms,
                directions,
            )

        numerator, leftover_real, leftover_imaginary = lax.map(
            pair_step, jnp.arange(pair_total, dtype=jnp.int32)
        )
        numerator = jnp.sum(numerator.reshape(shard_slots, shard_channels, -1), axis=1)
        numer_sum = reduce_normals(numerator)
        update = updated_field(current, numer_sum, denom_sum)
        target = select_points(
            update.reshape(shard_slots, station_list, sources), one_station, one_direction
        )
        partial_value = eigen_weight[None, :] * jnp.dot(target, eigen_basis, precision=HIGHEST)
        raw = lax.psum(partial_value, "chan")
        smooth = smooth_coefficients(raw)
        screen_own = jnp.dot(smooth, eigen_basis.T, precision=HIGHEST)
        placed = place_points(screen_own, one_station, one_direction).reshape(shard_slots, -1)
        tec_flat = lax.psum(placed, "chan")
    final_residual_real = leftover_real.reshape(shard_slots, shard_channels, baseline_list)
    final_residual_imaginary = leftover_imaginary.reshape(
        shard_slots, shard_channels, baseline_list
    )
    return (
        tec_flat.reshape(shard_slots, station_list, sources),
        smooth,
        final_residual_real,
        final_residual_imaginary,
    )


def solution(mesh):
    in_specs = (
        P("slot", "chan", None),
        P("slot", "chan", None),
        P("slot", "chan", None),
        P("slot", None, None),
        P(),
        P(),
        P("chan", None),
        P("chan"),
        P("slot", None, None),
        P("slot", None),
        P("chan", None),
        P(),
    )
    out_specs = (
        P("slot", None, None),
        P("slot", None),
        P("slot", "chan", None),
        P("slot", "chan", None),
    )
    return jax.shard_map(
        per_device, mesh=mesh, in_specs=in_specs, out_specs=out_specs, check_vma=False
    )
```

profile of v0, /device:TPU:0, one launch (start us, length us, event | category | flops | bytes accessed | tf_op | source)
XLA Modules:
  0.0 784.5 jit_solution(13449369649280400998)
XLA Ops:
  16.9 6.5 fusion.21
  23.4 6.8 fusion.32
  31.9 90.9 %all-reduce.3.cloned.1.call-done = (f32[1,12000]{1,0:T(1,128)}, f32[1,12000]{1,0:T(1,128)}) async-done(((f32[1,12000]{1,0:T(1,128)}, f32[1,12000]{1,0:T(1,128)}), (f32[1,12000]{1,0:T(1,128)}, f32[1,12000]{1,0:T(1,128)})) %all-reduce.3.cloned.1.call-update) | async-done | bytes 96016 | tf_op jit(solution)/shard_map/psum | solution.py:73
  124.5 5.7 fusion.155
  130.2 31.0 %psum.93 = f32[1,2048]{1,0:T(1,128)S(1)} all-reduce(f32[1,2048]{1,0:T(1,128)S(1)} %bitcast.100), channel_id=1, replica_groups=mesh['chan'=16,'slot'=2] {'chan'}, use_global_device_ids=true, to_apply=%region_5.6 | all-reduce | flops 2048 | bytes 16384 | tf_op jit(solution)/shard_map/psum | solution.py:164
  162.6 4.5 collective-permute-start
  168.4 7.1 convolution_reduce_fusion.3
  176.2 57.9 %psum.94 = f32[1,12000]{1,0:T(1,128)S(1)} all-reduce(f32[1,12000]{1,0:T(1,128)S(1)} %reshape.689), channel_id=1, replica_groups=mesh['chan'=16,'slot'=2] {'chan'}, use_global_device_ids=true, to_apply=%region_6.7 | all-reduce | flops 12000 | bytes 96000 | tf_op jit(solution)/shard_map/psum | solution.py:168
  234.4 6.5 fusion.23
  240.9 7.0 fusion.35
  248.1 57.7 %psum.95 = f32[1,12000]{1,0:T(1,128)S(1)} all-reduce(f32[1,12000]{1,0:T(1,128)S(1)} %reduce_sum.150), channel_id=1, replica_groups=mesh['chan'=16,'slot'=2] {'chan'}, use_global_device_ids=true, to_apply=%region_9.10 | all-reduce | flops 12000 | bytes 96000 | tf_op jit(solution)/shard_map/psum | solution.py:73
  306.6 5.7 fusion.156
  312.4 30.0 %psum.96 = f32[1,2048]{1,0:T(1,128)S(1)} all-reduce(f32[1,2048]{1,0:T(1,128)S(1)} %bitcast.101), channel_id=1, replica_groups=mesh['chan'=16,'slot'=2] {'chan'}, use_global_device_ids=true, to_apply=%region_11.12 | all-reduce | flops 2048 | bytes 16384 | tf_op jit(solution)/shard_map/psum | solution.py:164
  343.6 4.5 collective-permute-start.2
  349.5 7.1 convolution_reduce_fusion.2
  357.3 57.9 %psum.97 = f32[1,12000]{1,0:T(1,128)S(1)} all-reduce(f32[1,12000]{1,0:T(1,128)S(1)} %reshape.692), channel_id=1, replica_groups=mesh['chan'=16,'slot'=2] {'chan'}, use_global_device_ids=true, to_apply=%region_12.13 | all-reduce | flops 12000 | bytes 96000 | tf_op jit(solution)/shard_map/psum | solution.py:168
  415.5 6.5 fusion.25
  422.0 6.8 fusion.38
  428.9 57.7 %psum.98 = f32[1,12000]{1,0:T(1,128)S(1)} all-reduce(f32[1,12000]{1,0:T(1,128)S(1)} %reduce_sum.154), channel_id=1, replica_groups=mesh['chan'=16,'slot'=2] {'chan'}, use_global_device_ids=true, to_apply=%region_15.16 | all-reduce | flops 12000 | bytes 96000 | tf_op jit(solution)/shard_map/psum | solution.py:73
  487.5 5.7 fusion.157
  493.2 30.0 %psum.99 = f32[1,2048]{1,0:T(1,128)S(1)} all-reduce(f32[1,2048]{1,0:T(1,128)S(1)} %bitcast.102), channel_id=1, replica_groups=mesh['chan'=16,'slot'=2] {'chan'}, use_global_device_ids=true, to_apply=%region_17.18 | all-reduce | flops 2048 | bytes 16384 | tf_op jit(solution)/shard_map/psum | solution.py:164
  524.5 4.5 collective-permute-start.4
  530.4 7.1 convolution_reduce_fusion.1
  538.2 58.1 %psum.100 = f32[1,12000]{1,0:T(1,128)S(1)} all-reduce(f32[1,12000]{1,0:T(1,128)S(1)} %reshape.695), channel_id=1, replica_groups=mesh['chan'=16,'slot'=2] {'chan'}, use_global_device_ids=true, to_apply=%region_18.19 | all-reduce | flops 12000 | bytes 96000 | tf_op jit(solution)/shard_map/psum | solution.py:168
  596.5 6.5 fusion.27
  603.1 6.8 fusion.41
  610.0 57.7 %psum.101 = f32[1,12000]{1,0:T(1,128)S(1)} all-reduce(f32[1,12000]{1,0:T(1,128)S(1)} %reduce_sum.158), channel_id=1, replica_groups=mesh['chan'=16,'slot'=2] {'chan'}, use_global_device_ids=true, to_apply=%region_21.22 | all-reduce | flops 12000 | bytes 96000 | tf_op jit(solution)/shard_map/psum | solution.py:73
  668.5 5.7 fusion.158
  674.3 30.0 %psum.102 = f32[1,2048]{1,0:T(1,128)S(1)} all-reduce(f32[1,2048]{1,0:T(1,128)S(1)} %bitcast.103), channel_id=1, replica_groups=mesh['chan'=16,'slot'=2] {'chan'}, use_global_device_ids=true, to_apply=%region_23.24 | all-reduce | flops 2048 | bytes 16384 | tf_op jit(solution)/shard_map/psum | solution.py:164
  705.6 4.5 collective-permute-start.6
  711.5 7.1 convolution_reduce_fusion
  719.1 57.7 %psum.103 = f32[1,60,200]{2,1,0:T(8,128)S(1)} all-reduce(f32[1,60,200]{2,1,0:T(8,128)S(1)} %convolution_bitcast_fusion), channel_id=1, replica_groups=mesh['chan'=16,'slot'=2] {'chan'}, use_global_device_ids=true, to_apply=%region_24.25 | all-reduce | flops 12000 | bytes 96000 | tf_op jit(solution)/shard_map/psum | solution.py:168
  (88 shorter events, 29.6 us)
Async XLA Ops:
  7.2 7.6 copy-start
  7.2 9.7 %copy-start.3 = (f32[1,200]{1,0:T(1,128)S(1)}, f32[1,200]{1,0:T(1,128)}, u32[]{:S(2)}) copy-start(f32[1,200]{1,0:T(1,128)} %param.18) | copy-start | bytes 2404
  7.2 115.7 %all-reduce.3.cloned.1.call-start = ((), (), s32[]{:S(2)}) async-start(), calls=%async_computation | async-start | bytes 192512 | tf_op jit(solution)/shard_map/psum | solution.py:73
  124.5 5.8 copy-start.2
  161.3 5.9 collective-permute-start.1
  162.6 5.9 collective-permute-start
  240.9 64.9 %copy-start.1 = (f32[1,12000]{1,0:T(1,128)S(1)}, f32[1,12000]{1,0:T(1,128)}, u32[]{:S(2)}) copy-start(f32[1,12000]{1,0:T(1,128)} %get-tuple-element.141) | copy-start | bytes 144004
  342.3 5.9 collective-permute-start.3
  343.6 5.9 collective-permute-start.2
  523.2 5.9 collective-permute-start.5
  524.5 5.9 collective-permute-start.4
  668.5 41.6 %copy-start.5 = (f32[1,1,1770]{2,1,0:T(1,128)S(1)}, f32[1,1,1770]{2,1,0:T(1,128)}, u32[]{:S(2)}) copy-start(f32[1,1,1770]{2,1,0:T(1,128)} %param.12) | copy-start | bytes 21244
  668.5 41.6 %copy-start.6 = (f32[1,1,1770]{2,1,0:T(1,128)S(1)}, f32[1,1,1770]{2,1,0:T(1,128)}, u32[]{:S(2)}) copy-start(f32[1,1,1770]{2,1,0:T(1,128)} %param.13) | copy-start | bytes 21244
  704.3 6.5 collective-permute-start.7
  705.6 5.9 collective-permute-start.6
  711.5 7.1 copy-start.4
Sparse Core Ops, SparseCore 0:
  31.1 91.7 all-reduce.2
where the time goes:
time: 794 us; the launch traced here: 785 us
  blocking collectives  526 us (66%)
  matrix products  112 us (14%)
  waiting for transfers between devices  95.7 us (12%)
  starting transfers between devices  23.4 us (3%)
  between operations  15.5 us (2%)
    psum x4, blocking collectives, per_device(): tec_flat = lax.psum(placed, 'chan')  232 us
    psum x3, blocking collectives, reduce_normals(): return lax.psum(values, 'chan')  173 us
    psum x4, blocking collectives, per_device(): raw = lax.psum(partial_value, 'chan')  121 us
    psum x1, waiting for transfers between devices, reduce_normals(): return lax.psum(values, 'chan')  90.9 us
    dot_general x4, matrix products, per_device(): screen_own = jnp.dot(smooth, eigen_basis.T, precision=HIGHEST)  28.3 us
    dot_general x4, matrix products, pair_terms(): jnp.dot(signed_terms, projected, precision=HIGHEST)  27.3 us
    dot_general x4, matrix products, pair_terms(): jnp.dot(signed_terms.T, station_phase, precision=HIGHEST)  26 us
    dot_general x4, matrix products, per_device(): jnp.dot(target, eigen_basis, precision=HIGHEST)  23 us
  transfers between devices with their start and end apart: 9, of which 5 were waited for; matrix products, arithmetic and copies ran while one was open for 0% of the time, Pallas kernels for 0%

commit v1 on v0

--- a/solution.py
+++ b/solution.py
@@ -161,7 +161,7 @@
             update.reshape(shard_slots, station_list, sources), one_station, one_direction
         )
         partial_value = eigen_weight[None, :] * jnp.dot(target, eigen_basis, precision=HIGHEST)
-        raw = lax.psum(partial_value, "chan")
+        raw = jnp.sum(lax.all_gather(partial_value, "chan"), axis=0)
         smooth = smooth_coefficients(raw)
         screen_own = jnp.dot(smooth, eigen_basis.T, precision=HIGHEST)
         placed = place_points(screen_own, one_station, one_direction).reshape(shard_slots, -1)

time: 794 us -> 747 us (0.941)
  blocking collectives: 526 us -> 479 us
    psum x4 -> x0, blocking collectives: 121 us -> none  [per_device(): raw = lax.psum(partial_value, 'chan')]
    all_gather x0 -> x4, blocking collectives: none -> 72.1 us  [per_device(): raw = jnp.sum(lax.all_gather(partial_value, 'chan'), axis=0)]
where the time goes in v1:
time: 747 us; the launch traced here: 738 us
  blocking collectives  479 us (64%)
  matrix products  112 us (15%)
  waiting for transfers between devices  95.7 us (13%)
  starting transfers between devices  23.4 us (3%)
  between operations  15.5 us (2%)
    psum x4, blocking collectives, per_device(): tec_flat = lax.psum(placed, 'chan')  234 us
    psum x3, blocking collectives, reduce_normals(): return lax.psum(values, 'chan')  173 us
    psum x1, waiting for transfers between devices, reduce_normals(): return lax.psum(values, 'chan')  90.9 us
    all_gather x4, blocking collectives, per_device(): raw = jnp.sum(lax.all_gather(partial_value, 'chan'), axis=0)  72.1 us
    dot_general x4, matrix products, per_device(): screen_own = jnp.dot(smooth, eigen_basis.T, precision=HIGHEST)  28.3 us
    dot_general x4, matrix products, pair_terms(): jnp.dot(signed_terms, projected, precision=HIGHEST)  27.3 us
    dot_general x4, matrix products, pair_terms(): jnp.dot(signed_terms.T, station_phase, precision=HIGHEST)  26 us
    dot_general x4, matrix products, per_device(): jnp.dot(target, eigen_basis, precision=HIGHEST)  23 us
  transfers between devices with their start and end apart: 9, of which 5 were waited for; matrix products, arithmetic and copies ran while one was open for 0% of the time, Pallas kernels for 0%

profile of v1, /device:TPU:0, one launch (start us, length us, event | category | flops | bytes accessed | tf_op | source)
XLA Modules:
  0.0 737.9 jit_solution(9019870572987202442)
XLA Ops:
  16.9 6.5 fusion.21
  23.4 6.8 fusion.32
  31.9 90.9 %all-reduce.3.cloned.1.call-done = (f32[1,12000]{1,0:T(1,128)}, f32[1,12000]{1,0:T(1,128)}) async-done(((f32[1,12000]{1,0:T(1,128)}, f32[1,12000]{1,0:T(1,128)}), (f32[1,12000]{1,0:T(1,128)}, f32[1,12000]{1,0:T(1,128)})) %all-reduce.3.cloned.1.call-update) | async-done | bytes 96016 | tf_op jit(solution)/shard_map/psum | solution.py:73
  124.5 5.7 fusion.155
  130.2 19.8 %all-gather = f32[32768]{0:T(1024)S(1)} all-gather(f32[2048]{0:T(1024)S(1)} %mul.443), channel_id=2, replica_groups=mesh['chan'=16,'slot'=2] {'chan'}, dimensions={0}, use_global_device_ids=true | all-gather | bytes 139264 | tf_op jit(solution)/shard_map/all_gather | solution.py:164
  151.3 4.5 collective-permute-start
  157.2 7.1 convolution_reduce_fusion.3
  165.0 57.9 %psum.65 = f32[1,12000]{1,0:T(1,128)S(1)} all-reduce(f32[1,12000]{1,0:T(1,128)S(1)} %reshape.697), channel_id=1, replica_groups=mesh['chan'=16,'slot'=2] {'chan'}, use_global_device_ids=true, to_apply=%region_6.7 | all-reduce | flops 12000 | bytes 96000 | tf_op jit(solution)/shard_map/psum | solution.py:168
  223.2 6.5 fusion.23
  229.7 7.0 fusion.35
  236.8 57.7 %psum.66 = f32[1,12000]{1,0:T(1,128)S(1)} all-reduce(f32[1,12000]{1,0:T(1,128)S(1)} %reduce_sum.196), channel_id=1, replica_groups=mesh['chan'=16,'slot'=2] {'chan'}, use_global_device_ids=true, to_apply=%region_9.10 | all-reduce | flops 12000 | bytes 96000 | tf_op jit(solution)/shard_map/psum | solution.py:73
  295.4 5.7 fusion.156
  301.1 17.5 %all-gather.1 = f32[32768]{0:T(1024)S(1)} all-gather(f32[2048]{0:T(1024)S(1)} %mul.462), channel_id=3, replica_groups=mesh['chan'=16,'slot'=2] {'chan'}, dimensions={0}, use_global_device_ids=true | all-gather | bytes 139264 | tf_op jit(solution)/shard_map/all_gather | solution.py:164
  320.0 4.5 collective-permute-start.2
  325.9 7.1 convolution_reduce_fusion.2
  333.6 58.6 %psum.67 = f32[1,12000]{1,0:T(1,128)S(1)} all-reduce(f32[1,12000]{1,0:T(1,128)S(1)} %reshape.700), channel_id=1, replica_groups=mesh['chan'=16,'slot'=2] {'chan'}, use_global_device_ids=true, to_apply=%region_12.13 | all-reduce | flops 12000 | bytes 96000 | tf_op jit(solution)/shard_map/psum | solution.py:168
  392.4 6.5 fusion.25
  399.0 6.8 fusion.38
  405.9 57.7 %psum.68 = f32[1,12000]{1,0:T(1,128)S(1)} all-reduce(f32[1,12000]{1,0:T(1,128)S(1)} %reduce_sum.202), channel_id=1, replica_groups=mesh['chan'=16,'slot'=2] {'chan'}, use_global_device_ids=true, to_apply=%region_15.16 | all-reduce | flops 12000 | bytes 96000 | tf_op jit(solution)/shard_map/psum | solution.py:73
  464.4 5.7 fusion.157
  470.2 17.5 %all-gather.2 = f32[32768]{0:T(1024)S(1)} all-gather(f32[2048]{0:T(1024)S(1)} %mul.478), channel_id=4, replica_groups=mesh['chan'=16,'slot'=2] {'chan'}, dimensions={0}, use_global_device_ids=true | all-gather | bytes 139264 | tf_op jit(solution)/shard_map/all_gather | solution.py:164
  489.0 4.5 collective-permute-start.4
  494.9 7.1 convolution_reduce_fusion.1
  502.7 58.8 %psum.69 = f32[1,12000]{1,0:T(1,128)S(1)} all-reduce(f32[1,12000]{1,0:T(1,128)S(1)} %reshape.703), channel_id=1, replica_groups=mesh['chan'=16,'slot'=2] {'chan'}, use_global_device_ids=true, to_apply=%region_18.19 | all-reduce | flops 12000 | bytes 96000 | tf_op jit(solution)/shard_map/psum | solution.py:168
  561.7 6.5 fusion.27
  568.3 6.8 fusion.41
  575.2 57.7 %psum.70 = f32[1,12000]{1,0:T(1,128)S(1)} all-reduce(f32[1,12000]{1,0:T(1,128)S(1)} %reduce_sum.208), channel_id=1, replica_groups=mesh['chan'=16,'slot'=2] {'chan'}, use_global_device_ids=true, to_apply=%region_21.22 | all-reduce | flops 12000 | bytes 96000 | tf_op jit(solution)/shard_map/psum | solution.py:73
  633.7 5.7 fusion.158
  639.5 17.5 %all-gather.3 = f32[32768]{0:T(1024)S(1)} all-gather(f32[2048]{0:T(1024)S(1)} %mul.494), channel_id=5, replica_groups=mesh['chan'=16,'slot'=2] {'chan'}, dimensions={0}, use_global_device_ids=true | all-gather | bytes 139264 | tf_op jit(solution)/shard_map/all_gather | solution.py:164
  658.3 4.5 collective-permute-start.6
  664.2 7.1 convolution_reduce_fusion
  671.9 58.4 %psum.71 = f32[1,60,200]{2,1,0:T(8,128)S(1)} all-reduce(f32[1,60,200]{2,1,0:T(8,128)S(1)} %convolution_bitcast_fusion), channel_id=1, replica_groups=mesh['chan'=16,'slot'=2] {'chan'}, use_global_device_ids=true, to_apply=%region_24.25 | all-reduce | flops 12000 | bytes 96000 | tf_op jit(solution)/shard_map/psum | solution.py:168
  (96 shorter events, 29.8 us)
Async XLA Ops:
  7.2 7.6 %copy-start = (f32[3,200]{1,0:T(4,128)S(1)}, f32[3,200]{1,0:T(4,128)}, u32[]{:S(2)}) copy-start(f32[3,200]{1,0:T(4,128)} %param.17) | copy-start | bytes 7204
  7.2 9.7 %copy-start.3 = (f32[1,200]{1,0:T(1,128)S(1)}, f32[1,200]{1,0:T(1,128)}, u32[]{:S(2)}) copy-start(f32[1,200]{1,0:T(1,128)} %param.18) | copy-start | bytes 2404
  7.2 115.6 %all-reduce.3.cloned.1.call-start = ((), (), s32[]{:S(2)}) async-start(), calls=%async_computation | async-start | bytes 192512 | tf_op jit(solution)/shard_map/psum | solution.py:73
  124.4 5.8 copy-start.2
  150.0 5.9 collective-permute-start.1
  151.3 5.9 collective-permute-start
  229.7 64.9 %copy-start.1 = (f32[1,12000]{1,0:T(1,128)S(1)}, f32[1,12000]{1,0:T(1,128)}, u32[]{:S(2)}) copy-start(f32[1,12000]{1,0:T(1,128)} %get-tuple-element.158) | copy-start | bytes 144004
  318.7 5.9 collective-permute-start.3
  320.0 5.9 collective-permute-start.2
  487.7 5.9 collective-permute-start.5
  489.0 5.9 collective-permute-start.4
  633.7 29.2 %copy-start.5 = (f32[1,1,1770]{2,1,0:T(1,128)S(1)}, f32[1,1,1770]{2,1,0:T(1,128)}, u32[]{:S(2)}) copy-start(f32[1,1,1770]{2,1,0:T(1,128)} %param.12) | copy-start | bytes 21244
  633.7 29.2 %copy-start.6 = (f32[1,1,1770]{2,1,0:T(1,128)S(1)}, f32[1,1,1770]{2,1,0:T(1,128)}, u32[]{:S(2)}) copy-start(f32[1,1,1770]{2,1,0:T(1,128)} %param.13) | copy-start | bytes 21244
  657.0 6.5 collective-permute-start.7
  658.3 5.9 collective-permute-start.6
  664.2 7.1 copy-start.4
Sparse Core Ops, SparseCore 0:
  31.1 91.7 all-reduce.2
